TPU v7x, 128 devices: a whole 4x4x4 slice. The times are simulated.
128 devices in a mesh: tm: 4 (over x), panel: 32 (over y, z, core).
Axes of the slice: x: 4, y: 4, z: 4, core: 2. Of those that a mesh axis runs over, the one named last changes fastest.
Arguments:
- separator_cov: float32 [4, 2048, 2048], P('tm', 'panel'), may hold values from -6 to 6
- separator_arrow: float32 [4, 6, 2048], P('tm'), may hold values from -6 to 6
- coupling: float32 [4, 2048, 2048], P('tm', 'panel'), may hold values from -0.25 to 0.25
- arrow_factor: float32 [4, 6, 2048], P('tm'), may hold values from -6 to 6
- arrow_tip: float32 [6, 6], replicated, may hold values from -6 to 6
- inverse_gram: float32 [4, 2048, 2048], P('tm', 'panel'), may hold values from -6 to 6
Outputs:
- diag_cov: float32 [4, 2048, 2048], P('tm', 'panel')
- off_diag: float32 [4, 2048, 2048], P('tm', 'panel')
- arrow_cov: float32 [4, 6, 2048], P('tm', None, 'panel')
All inputs are finite; a program needn't handle non-finite values.
Results may differ from a plain program's by a relative error of at most 0.0001.
Values sent between devices are 32-bit elements; how exact they have to be, the bound alone decides.
No kernel may reach another device: no remote copies, remote signals or barrier semaphores. Data moves between devices by JAX's collectives and lax.ppermute only.
A program may use at most 128 MiB of HBM per device.

v0:
```python
import jax
import jax.numpy as jnp
from jax import lax
from jax.sharding import PartitionSpec as P

hp = lax.Precision.HIGHEST


def passed_along(block, axis, distance):
    devices = range(lax.axis_size(axis))
    route = [(i - distance, i) for i in devices if i - distance in devices]
    return lax.ppermute(block, axis, route)


def matmul(left, right):
    return jnp.dot(left, right, preferred_element_type=jnp.float32, precision=hp)


def inner_rows(left, right):
    return lax.dot_general(
        left, right, (((0,), (0,)), ((), ())), preferred_element_type=jnp.float32, precision=hp
    )


def per_device(separator_cov, separator_arrow, coupling, arrow_factor, arrow_tip, inverse_gram):
    next_cov, next_arrow = passed_along((separator_cov[0], separator_arrow[0]), "tm", -1)
    factor = coupling[0]
    arrow_rows = arrow_factor[0]
    height = factor.shape[0]
    offset = lax.axis_index("panel") * height
    product = matmul(next_cov, lax.all_gather(factor, "panel", axis=0, tiled=True))
    mine_arrow = lax.dynamic_slice_in_dim(next_arrow, offset, height, 1)
    arrow_prod = lax.psum(matmul(mine_arrow, factor), "panel")
    arrow_out = -(arrow_prod + matmul(arrow_tip, arrow_rows))
    own_next_arrow = lax.dynamic_slice_in_dim(next_arrow, offset, height, 1)
    lower = -(product + inner_rows(own_next_arrow, arrow_rows))
    folded = lax.psum_scatter(inner_rows(factor, lower), "panel", scatter_dimension=0, tiled=True)
    own_arrow_rows = lax.dynamic_slice_in_dim(arrow_rows, offset, height, 1)
    diag_out = inverse_gram[0] - folded - inner_rows(own_arrow_rows, arrow_out)
    arrow_share = lax.dynamic_slice_in_dim(arrow_out, offset, height, 1)
    return (diag_out[None], lower[None], arrow_share[None])


def solution(mesh):
    return jax.shard_map(
        per_device,
        mesh=mesh,
        in_specs=(
            P("tm", "panel", None),
            P("tm", None, None),
            P("tm", "panel", None),
            P("tm", None, None),
            P(),
            P("tm", "panel", None),
        ),
        out_specs=(P("tm", "panel", None), P("tm", "panel", None), P("tm", None, "panel")),
        check_vma=False,
    )
```

profile of v0, /device:TPU:0, one launch (start us, length us, event | category | flops | bytes accessed | tf_op | source)
XLA Modules:
  0.0 272.7 jit_solution(7942340729840633537)
XLA Ops:
  7.2 0.0 copy-start
  7.2 0.0 all-gather.3.cloned.1.call-start
  7.2 0.7 all-gather.3.cloned.1.call-update
  7.9 0.0 reduce-scatter.4.cloned.1.call-start
  8.0 1.3 collective-permute-start
  9.3 0.8 copy.31
  10.1 1.3 collective-permute-start.1
  11.4 13.6 %collective-permute-done.1 = f32[6,2048]{1,0:T(8,128)S(1)} collective-permute-done((f32[6,2048]{1,0:T(8,128)S(1)}, f32[6,2048]{1,0:T(8,128)S(1)}, u32[]{:S(2)}, u32[]{:S(2)}) %collective-permute-start.1) | collective-permute-done | bytes 49184 | tf_op jit(solution)/shard_map/ppermute | solution.py:12
  25.0 1.5 fusion.14
  26.5 0.0 collective-permute-done
  26.5 58.9 %all-gather.3.cloned.1.call-done = f32[1,2048,2048]{2,1,0:T(8,128)} async-done(((f32[1,64,2048]{2,1,0:T(8,128)}), f32[1,2048,2048]{2,1,0:T(8,128)}) %all-gather.3.cloned.1.call-update) | async-done | bytes 16777232 | tf_op jit(solution)/shard_map/all_gather | solution.py:31
  85.5 13.8 %fusion.6 = f32[64,2048]{1,0:T(8,128)S(1)} fusion(f32[64,2048]{1,0:T(8,128)S(1)} %fusion.14, f32[64,2048]{1,0:T(8,128)S(1)} %collective-permute-done, f32[1,2048,2048]{2,1,0:T(8,128)} %all-gather.3.cloned.1.call-done), kind=kOutput, calls=%fused_computation.6 | convolution fusion | flops 3221487616 | bytes 18350080 | tf_op jit(solution)/shard_map/dot_general | solution.py:16
  99.3 0.0 copy-start.2
  99.3 16.0 %convolution_bitcast_fusion = f32[2048,2048]{0,1:T(8,128)} fusion(f32[64,2048]{1,0:T(8,128)S(1)} %fusion.6, f32[1,64,2048]{2,1,0:T(8,128)S(1)} %copy-done.1), kind=kOutput, calls=%fused_computation.2 | convolution fusion | flops 3221225472 | bytes 17825792 | tf_op jit(solution)/shard_map/dot_general | solution.py:20
  115.3 17.6 %copy.13 = f32[2048,2048]{1,0:T(8,128)} copy(f32[2048,2048]{0,1:T(8,128)} %convolution_bitcast_fusion) | data formatting | bytes 33554432
  132.9 0.0 reduce-scatter.4.cloned.1.call-update
  132.9 0.8 copy-done.4
  133.7 0.1 constant_dynamic-slice_fusion.1
  133.8 0.2 fusion.12
  134.0 0.4 fusion.10
  134.4 128.3 %psum.7 = f32[6,2048]{1,0:T(8,128)S(1)} all-reduce(f32[6,2048]{1,0:T(8,128)S(1)} %fusion.10), channel_id=1, replica_groups=mesh['tm'=4,'panel'=32] {'panel'}, use_global_device_ids=true, to_apply=%region_1.0 | all-reduce | flops 12288 | bytes 98304 | tf_op jit(solution)/shard_map/psum | solution.py:33
  262.7 0.1 constant_dynamic-slice_fusion
  262.8 0.6 broadcast_in_dim.11
  263.4 2.5 fusion.2
  (9 shorter events, 0.0 us)
Async XLA Ops:
  7.2 126.6 %copy-start = (f32[6,6]{1,0:T(8,128)S(1)}, f32[6,6]{1,0:T(8,128)}, u32[]{:S(2)}) copy-start(f32[6,6]{1,0:T(8,128)} %param.10) | copy-start | bytes 436
  7.2 92.1 %copy-start.1 = (f32[1,64,2048]{2,1,0:T(8,128)S(1)}, f32[1,64,2048]{2,1,0:T(8,128)}, u32[]{:S(2)}) copy-start(f32[1,64,2048]{2,1,0:T(8,128)} %param.8) | copy-start | bytes 1572868
  7.2 78.3 %all-gather.3.cloned.1.call-start = ((), (), s32[]{:S(2)}) async-start(), calls=%async_computation.1 | async-start | bytes 17301504 | tf_op jit(solution)/shard_map/all_gather | solution.py:31
  7.9 255.4 %reduce-scatter.4.cloned.1.call-start = ((), (), s32[]{:S(2)}) async-start(), calls=%async_computation.2 | async-start | bytes 17301504 | tf_op jit(solution)/shard_map/reduce_scatter | solution.py:37
  8.0 18.6 %collective-permute-start = (f32[64,2048]{1,0:T(8,128)}, f32[64,2048]{1,0:T(8,128)S(1)}, u32[]{:S(2)}, u32[]{:S(2)}) collective-permute-start(f32[64,2048]{1,0:T(8,128)} %bitcast.40), channel_id=1, source_target_pairs={{32,0},{64,32},{96,64},{33,1},{65,33},{97,65},{34,2},{66,34},{98,6... | collective-permute-start | bytes 1572872 | tf_op jit(solution)/shard_map/ppermute | solution.py:12
  10.1 14.9 %collective-permute-start.1 = (f32[6,2048]{1,0:T(8,128)S(1)}, f32[6,2048]{1,0:T(8,128)S(1)}, u32[]{:S(2)}, u32[]{:S(2)}) collective-permute-start(f32[6,2048]{1,0:T(8,128)S(1)} %bitcast.39), channel_id=1, source_target_pairs={{32,0},{64,32},{96,64},{33,1},{65,33},{97,65},{34,2},{66,34},{98,6... | collective-permute-start | bytes 147464 | tf_op jit(solution)/shard_map/ppermute | solution.py:12
  99.3 33.6 %copy-start.2 = (f32[64,2048]{1,0:T(8,128)}, f32[64,2048]{1,0:T(8,128)S(1)}, u32[]{:S(2)}) copy-start(f32[64,2048]{1,0:T(8,128)S(1)} %fusion.6) | copy-start | bytes 1572868
  132.9 0.8 copy-start.4
  132.9 130.5 %copy-start.3 = (f32[1,64,2048]{2,1,0:T(8,128)S(1)}, f32[1,64,2048]{2,1,0:T(8,128)}, u32[]{:S(2)}) copy-start(f32[1,64,2048]{2,1,0:T(8,128)} %param.11) | copy-start | bytes 1572868
Sparse Core Ops, SparseCore 0:
  10.3 75.1 all-gather.2
  133.1 115.5 reduce-scatter.3
where the time goes:
time: 273 us
  blocking collectives  128 us (47%)
  waiting for transfers between devices  73.2 us (27%)
  matrix products  34.4 us (13%)
  local copies, waits for them, and re-layouts  19.9 us (7%)
  between operations  14.1 us (5%)
    psum x1, blocking collectives, per_device(): arrow_prod = lax.psum(matmul(mine_arrow, factor), 'panel')  128 us
    all_gather x1, waiting for transfers between devices, per_device(): lax.all_gather(factor, 'panel', axis=0, tiled=True)  58.9 us
    dot_general x3, matrix products, inner_rows(): lax.dot_general(left, right, (((0,), (0,)), ((), ())), preferred_element_...  20 us
    unnamed x12, local copies, waits for them, and re-layouts  19.2 us
    dot_general x3, matrix products, matmul(): jnp.dot(left, right, preferred_element_type=jnp.float32, precision=hp)  14.4 us
    ppermute x2, waiting for transfers between devices, passed_along(): return lax.ppermute(block, axis, route)  13.6 us
  transfers between devices with their start and end apart: 4, of which 2 were waited for; matrix products, arithmetic and copies ran while one was open for 1% of the time, Pallas kernels for 0%

commit v1 on v0

--- a/solution.py
+++ b/solution.py
@@ -28,7 +28,12 @@
     arrow_rows = arrow_factor[0]
     height = factor.shape[0]
     offset = lax.axis_index("panel") * height
-    product = matmul(next_cov, lax.all_gather(factor, "panel", axis=0, tiled=True))
+    product = matmul(
+        next_cov,
+        jnp.concatenate(
+            lax.all_to_all(jnp.stack([factor] * lax.axis_size("panel")), "panel", 0, 0), axis=0
+        ),
+    )
     mine_arrow = lax.dynamic_slice_in_dim(next_arrow, offset, height, 1)
     arrow_prod = lax.psum(matmul(mine_arrow, factor), "panel")
     arrow_out = -(arrow_prod + matmul(arrow_tip, arrow_rows))

time: 273 us -> 473 us (1.73)
  waiting for transfers between devices: 73.2 us -> 237 us
  blocking collectives: 128 us -> 149 us
  starting transfers between devices: 2.66 us -> 11.5 us
  local copies, waits for them, and re-layouts: 19.9 us -> 27.4 us
    all_to_all x0 -> x1, waiting for transfers between devices: none -> 222 us  [per_device(): lax.all_to_all(jnp.stack([factor] * lax.axis_size('panel')), 'panel', 0, 0)]
    all_gather x1 -> x0, waiting for transfers between devices: 58.9 us -> none  [per_device(): lax.all_gather(factor, 'panel', axis=0, tiled=True)]
    psum x1, blocking collectives: 128 us -> 149 us  [per_device(): arrow_prod = lax.psum(matmul(mine_arrow, factor), 'panel')]
    another operation x0 -> x1, local copies, waits for them, and re-layouts: none -> 8.93 us  [per_device(): jnp.stack([factor] * lax.axis_size('panel'))]
    all_to_all x0 -> x1, starting transfers between devices: none -> 8.71 us  [per_device(): lax.all_to_all(jnp.stack([factor] * lax.axis_size('panel')), 'panel', 0, 0)]
    unnamed x12 -> x16, local copies, waits for them, and re-layouts: 19.2 us -> 17.7 us
  transfers between devices with their start and end apart: 4 -> 4, of which waited for: 2 -> 2; matrix products, arithmetic and copies ran while one was open for 1% -> 0% of each run, Pallas kernels for 0% -> 0%
where the time goes in v1:
time: 473 us
  waiting for transfers between devices  237 us (50%)
  blocking collectives  149 us (32%)
  matrix products  33.7 us (7%)
  local copies, waits for them, and re-layouts  27.4 us (6%)
  between operations  14.2 us (3%)
  starting transfers between devices  11.5 us (2%)
    all_to_all x1, waiting for transfers between devices, per_device(): lax.all_to_all(jnp.stack([factor] * lax.axis_size('panel')), 'panel', 0, 0)  222 us
    psum x1, blocking collectives, per_device(): arrow_prod = lax.psum(matmul(mine_arrow, factor), 'panel')  149 us
    dot_general x3, matrix products, inner_rows(): lax.dot_general(left, right, (((0,), (0,)), ((), ())), preferred_element_...  19.3 us
    unnamed x16, local copies, waits for them, and re-layouts  17.7 us
    ppermute x2, waiting for transfers between devices, passed_along(): return lax.ppermute(block, axis, route)  14.7 us
    dot_general x3, matrix products, matmul(): jnp.dot(left, right, preferred_element_type=jnp.float32, precision=hp)  14.4 us
  transfers between devices with their start and end apart: 4, of which 2 were waited for; matrix products, arithmetic and copies ran while one was open for 0% of the time, Pallas kernels for 0%

profile of v1, /device:TPU:0, one launch (start us, length us, event | category | flops | bytes accessed | tf_op | source)
XLA Modules:
  0.0 472.8 jit_solution(8523424194310628522)
XLA Ops:
  7.2 0.0 copy-start
  7.2 8.9 %stack.3 = f32[32,64,2048]{2,1,0:T(8,128)} broadcast(f32[64,2048]{1,0:T(8,128)} %bitcast.33), dimensions={1,2} | broadcast | bytes 17301504 | tf_op jit(solution)/shard_map/stack | solution.py:34
  16.1 8.7 %all-to-all-start = ((f32[32,64,2048]{2,1,0:T(8,128)}), f32[32,64,2048]{2,1,0:T(8,128)}, u32[]{:S(2)}, u32[]{:S(2)}) async-start(f32[32,64,2048]{2,1,0:T(8,128)} %stack.3), calls=%async_computation | async-start | bytes 33554432 | tf_op jit(solution)/shard_map/all_to_all | solution.py:34
  24.8 0.0 copy-start.1
  24.8 0.0 reduce-scatter.4.cloned.1.call-start
  24.9 1.4 collective-permute-start
  26.4 1.3 collective-permute-start.1
  27.7 14.7 %collective-permute-done.1 = f32[6,2048]{1,0:T(8,128)S(1)} collective-permute-done((f32[6,2048]{1,0:T(8,128)S(1)}, f32[6,2048]{1,0:T(8,128)S(1)}, u32[]{:S(2)}, u32[]{:S(2)}) %collective-permute-start.1) | collective-permute-done | bytes 49184 | tf_op jit(solution)/shard_map/ppermute | solution.py:12
  42.4 0.0 copy-done.4
  42.4 0.7 fusion.4
  43.1 0.0 collective-permute-done
  43.1 221.9 %all-to-all-done = f32[32,64,2048]{2,1,0:T(8,128)} async-done(((f32[32,64,2048]{2,1,0:T(8,128)}), f32[32,64,2048]{2,1,0:T(8,128)}, u32[]{:S(2)}, u32[]{:S(2)}) %all-to-all-start) | async-done | bytes 16777248 | tf_op jit(solution)/shard_map/all_to_all | solution.py:34
  265.0 13.8 %fusion.1 = f32[64,2048]{1,0:T(8,128)S(1)} fusion(f32[64,2048]{1,0:T(8,128)S(1)} %fusion.4, f32[64,2048]{1,0:T(8,128)S(1)} %collective-permute-done, f32[2048,2048]{1,0:T(8,128)} %bitcast.3), kind=kOutput, calls=%fused_computation.4 | convolution fusion | flops 3221487616 | bytes 18350080 | tf_op jit(solution)/shard_map/dot_general | solution.py:16
  278.9 0.0 copy-start.2
  278.9 16.1 %convolution_bitcast_fusion = f32[2048,2048]{0,1:T(8,128)} fusion(f32[64,2048]{1,0:T(8,128)S(1)} %fusion.1, f32[1,64,2048]{2,1,0:T(8,128)S(1)} %copy-done.1), kind=kOutput, calls=%fused_computation | convolution fusion | flops 3221225472 | bytes 17825792 | tf_op jit(solution)/shard_map/dot_general | solution.py:20
  295.0 17.6 %copy.13 = f32[2048,2048]{1,0:T(8,128)} copy(f32[2048,2048]{0,1:T(8,128)} %convolution_bitcast_fusion) | data formatting | bytes 33554432
  312.6 0.0 reduce-scatter.4.cloned.1.call-update
  312.7 0.1 constant_dynamic-slice_fusion.1
  312.7 0.2 fusion.2
  312.9 0.4 fusion.10
  313.3 149.5 %psum.7 = f32[6,2048]{1,0:T(8,128)S(1)} all-reduce(f32[6,2048]{1,0:T(8,128)S(1)} %fusion.10), channel_id=1, replica_groups=mesh['tm'=4,'panel'=32] {'panel'}, use_global_device_ids=true, to_apply=%region_1.0 | all-reduce | flops 12288 | bytes 98304 | tf_op jit(solution)/shard_map/psum | solution.py:38
  462.8 0.1 constant_dynamic-slice_fusion
  462.9 0.6 broadcast_in_dim.11
  463.4 2.5 fusion
  (13 shorter events, 0.1 us)
Async XLA Ops:
  7.2 305.6 %copy-start = (f32[6,6]{1,0:T(8,128)S(1)}, f32[6,6]{1,0:T(8,128)}, u32[]{:S(2)}) copy-start(f32[6,6]{1,0:T(8,128)} %param.10) | copy-start | bytes 436
  16.1 8.8 %copy-start.6 = (f32[1,64,2048]{2,1,0:T(8,128)S(1)}, f32[1,64,2048]{2,1,0:T(8,128)}, u32[]{:S(2)}) copy-start(f32[1,64,2048]{2,1,0:T(8,128)} %param.6) | copy-start | bytes 1572868
  16.1 10.2 %copy-start.5 = (f32[1,6,2048]{2,0,1:T(1,128)S(1)}, f32[1,6,2048]{2,0,1:T(1,128)}, u32[]{:S(2)}) copy-start(f32[1,6,2048]{2,0,1:T(1,128)} %param.7) | copy-start | bytes 147460
  16.1 26.2 %copy-start.4 = (f32[1,6,2048]{2,0,1:T(1,128)S(1)}, f32[1,6,2048]{2,0,1:T(1,128)}, u32[]{:S(2)}) copy-start(f32[1,6,2048]{2,0,1:T(1,128)} %param.9) | copy-start | bytes 147460
  16.1 248.9 %all-to-all-start = ((f32[32,64,2048]{2,1,0:T(8,128)}), f32[32,64,2048]{2,1,0:T(8,128)}, u32[]{:S(2)}, u32[]{:S(2)}) async-start(f32[32,64,2048]{2,1,0:T(8,128)} %stack.3), calls=%async_computation | async-start | bytes 33554432 | tf_op jit(solution)/shard_map/all_to_all | solution.py:34
  24.8 254.1 %copy-start.1 = (f32[1,64,2048]{2,1,0:T(8,128)S(1)}, f32[1,64,2048]{2,1,0:T(8,128)}, u32[]{:S(2)}) copy-start(f32[1,64,2048]{2,1,0:T(8,128)} %param.8) | copy-start | bytes 1572868
  24.8 438.6 %reduce-scatter.4.cloned.1.call-start = ((), (), s32[]{:S(2)}) async-start(), calls=%async_computation.2 | async-start | bytes 17301504 | tf_op jit(solution)/shard_map/reduce_scatter | solution.py:42
  24.9 18.2 %collective-permute-start = (f32[64,2048]{1,0:T(8,128)S(1)}, f32[64,2048]{1,0:T(8,128)S(1)}, u32[]{:S(2)}, u32[]{:S(2)}) collective-permute-start(f32[64,2048]{1,0:T(8,128)S(1)} %bitcast.36), channel_id=1, source_target_pairs={{32,0},{64,32},{96,64},{33,1},{65,33},{97,65},{34,2},{66,34},{98,6... | collective-permute-start | bytes 1572872 | tf_op jit(solution)/shard_map/ppermute | solution.py:12
  26.4 16.0 %collective-permute-start.1 = (f32[6,2048]{1,0:T(8,128)S(1)}, f32[6,2048]{1,0:T(8,128)S(1)}, u32[]{:S(2)}, u32[]{:S(2)}) collective-permute-start(f32[6,2048]{1,0:T(8,128)S(1)} %bitcast.35), channel_id=1, source_target_pairs={{32,0},{64,32},{96,64},{33,1},{65,33},{97,65},{34,2},{66,34},{98,6... | collective-permute-start | bytes 147464 | tf_op jit(solution)/shard_map/ppermute | solution.py:12
  278.9 33.7 %copy-start.2 = (f32[64,2048]{1,0:T(8,128)}, f32[64,2048]{1,0:T(8,128)S(1)}, u32[]{:S(2)}) copy-start(f32[64,2048]{1,0:T(8,128)S(1)} %fusion.1) | copy-start | bytes 1572868
  312.6 150.8 %copy-start.3 = (f32[1,64,2048]{2,1,0:T(8,128)S(1)}, f32[1,64,2048]{2,1,0:T(8,128)}, u32[]{:S(2)}) copy-start(f32[1,64,2048]{2,1,0:T(8,128)} %param.11) | copy-start | bytes 1572868
Sparse Core Ops, SparseCore 0:
  312.8 144.7 reduce-scatter.3
